TPU v7x, 32 devices: a whole 2x2x4 slice. The times are simulated.
32 devices in a mesh: branch: 2 (over y), res: 16 (over z, x, core).
Axes of the slice: x: 2, y: 2, z: 4, core: 2. Of those that a mesh axis runs over, the one named last changes fastest.
Arguments:
- alignment_representation: float32 [128, 96, 256], P(None, 'res'), may hold values from -6 to 6
- pairwise_state: float32 [96, 96, 128], P('res'), may hold values from -6 to 6
- alignment_mask: int32 [128, 96], P(None, 'res'), may hold values from 0 to 1, as said below
- residue_present_mask: int32 [96], P('res'), may hold values from 0 to 1, as said below
- row_projection_weight: float32 [4, 256, 256], replicated
- lateral_result_coeffs: float32 [256, 256], replicated, may hold values from -1.5 to 1.5
- pair_bias_weight: float32 [128, 8], replicated, may hold values from -0.75 to 0.75
- first_operand_coeffs: float32 [256, 32], replicated, may hold values from -0.375 to 0.375
- other_operand_coeffs: float32 [256, 32], replicated, may hold values from -0.375 to 0.375
- outer_output_weight: float32 [1024, 128], replicated, may hold values from -2 to 2
- starting_projection_weight: float32 [4, 128, 128], replicated
- starting_bias_weight: float32 [128, 4], replicated, may hold values from -0.75 to 0.75
- starting_output_weight: float32 [128, 128], replicated, may hold values from -2 to 2
- ending_projection_weight: float32 [4, 128, 128], replicated
- ending_bias_weight: float32 [128, 4], replicated, may hold values from -0.75 to 0.75
- ending_output_weight: float32 [128, 128], replicated, may hold values from -2 to 2
Outputs:
- alignment_output: float32 [128, 96, 256], P('branch', 'res')
- pairwise_output: float32 [96, 96, 128], P('res', None, 'branch')
Inputs may be any that keep to these rules, and one draw needn't show every extreme that they name: residue_present_mask is 1 on the first L residues and 0 on the rest, for a drawn L from 48 to 96. alignment_mask[s, r] is 1 exactly where s is below a drawn count from 32 to 128 and residue_present_mask[r] is 1.
All inputs are finite; a program needn't handle non-finite values.
Results may differ from a plain program's by a relative error of at most 0.0003.
Values sent between devices are 32-bit elements; how exact they have to be, the bound alone decides.
A program may use at most 128 MiB of HBM per device.

v0:
```python
import math
import jax
import jax.numpy as jnp
from jax import lax
from jax.sharding import PartitionSpec as P

ATTEND_HEADS = 8
HEADS_Z = 4
highest = lax.Precision.HIGHEST
epsilon = 1e-05
masked_score = -1000000000.0


def spread(value, axis, root):
    mine = lax.axis_index(axis) == root
    return lax.psum(jnp.where(mine, value, jnp.zeros_like(value)), axis)


def partner(block, axis, apart):
    count = lax.axis_size(axis)
    route = []
    for low in range(count):
        high = low | 1 << apart
        if high != low and high < count:
            route += [(low, high), (high, low)]
    return lax.ppermute(block, axis, route)


def layer_normalize(values):
    centred = values - jnp.mean(values, axis=-1, keepdims=True)
    variance = jnp.mean(centred * centred, axis=-1, keepdims=True)
    return centred * lax.rsqrt(variance + epsilon)


def linear_project(values, weight):
    return jnp.dot(values, weight, precision=highest, preferred_element_type=jnp.float32)


def attend(query_matrix, key_matrix, value_matrix, gate_matrix, score_bias, live_keys, head_count):
    head_width = query_matrix.shape[-1] // head_count
    shaped_q = query_matrix.reshape(query_matrix.shape[0], head_count, head_width)
    shaped_k = key_matrix.reshape(key_matrix.shape[0], head_count, head_width)
    shaped_v = value_matrix.reshape(value_matrix.shape[0], head_count, head_width)
    scores = (
        jnp.einsum("qhd,khd->hqk", shaped_q, shaped_k, precision=highest) / math.sqrt(head_width)
        + score_bias
    )
    scores = jnp.where(live_keys[None, None, :], scores, masked_score)
    scores = scores - jnp.max(scores, axis=-1, keepdims=True)
    weights = jnp.exp(scores)
    weights = weights / jnp.sum(weights, axis=-1, keepdims=True)
    mixture = jnp.einsum("hqk,khd->qhd", weights, shaped_v, precision=highest)
    return jax.nn.sigmoid(gate_matrix) * mixture.reshape(
        query_matrix.shape[0], head_count * head_width
    )


def factor_matrix(normed, float_mask, weight):
    return jnp.transpose(linear_project(normed, weight) * float_mask[:, :, None], (1, 2, 0))


def outer_block(left_matrix, mask_rows, right_all, mask_all, out_weight):
    residues, factor_width, sequences = right_all.shape

    def outer_one_row(operands):
        row_left, row_mask = operands
        outer_sum = jnp.einsum("cs,jes->jce", row_left, right_all, precision=highest)
        outer_sum = outer_sum.reshape(residues, factor_width * factor_width)
        intersection = jnp.einsum("ns,s->n", mask_all, row_mask, precision=highest)
        return linear_project(outer_sum, out_weight) / jnp.maximum(intersection, 1.0)[:, None]

    return lax.map(outer_one_row, (left_matrix, mask_rows))


def per_device(
    alignment_representation,
    pairwise_state,
    alignment_mask,
    residue_present_mask,
    row_projection_weight,
    lateral_result_coeffs,
    pair_bias_weight,
    first_operand_coeffs,
    other_operand_coeffs,
    outer_output_weight,
    starting_projection_weight,
    starting_bias_weight,
    starting_output_weight,
    ending_projection_weight,
    ending_bias_weight,
    ending_output_weight,
):
    alignment_present_flag = lax.axis_index("branch") == 0
    sequence_count = alignment_representation.shape[0]
    local_matrix = alignment_representation.shape[1]
    residues = pairwise_state.shape[1]
    pair_width = pairwise_state.shape[2]
    float_mask = alignment_mask.astype(jnp.float32)
    mask_rows = jnp.transpose(float_mask)
    update_dimensions = (local_matrix, residues, pair_width)

    def bias_rows_of(field):
        return jnp.einsum(
            "ijc,ch->hij", layer_normalize(field), pair_bias_weight, precision=highest
        )

    normed_alignment = layer_normalize(alignment_representation)
    handed = lax.cond(
        alignment_present_flag,
        lambda: jnp.zeros((pair_bias_weight.shape[1], local_matrix, residues), jnp.float32),
        lambda: bias_rows_of(pairwise_state),
    )
    own_rows = spread(handed, "branch", 1)
    row_bias = lax.all_gather(own_rows, "res", axis=1, tiled=True)
    seq_normed, seq_mask = (
        lax.all_to_all(normed_alignment, "res", split_axis=0, concat_axis=1, tiled=True),
        lax.all_to_all(float_mask, "res", split_axis=0, concat_axis=1, tiled=True),
    )

    def row_attention():
        query_matrix = linear_project(seq_normed, row_projection_weight[0])
        key_matrix = linear_project(seq_normed, row_projection_weight[1])
        value_matrix = linear_project(seq_normed, row_projection_weight[2])
        gate_matrix = linear_project(seq_normed, row_projection_weight[3])
        sequence_present = seq_mask > 0.5

        def one_sequence(operands):
            return attend(
                operands[0],
                operands[1],
                operands[2],
                operands[3],
                row_bias,
                operands[4],
                ATTEND_HEADS,
            )

        gated_output = lax.map(
            one_sequence, (query_matrix, key_matrix, value_matrix, gate_matrix, sequence_present)
        )
        return linear_project(gated_output, lateral_result_coeffs)

    row_change = lax.cond(alignment_present_flag, row_attention, lambda: jnp.zeros_like(seq_normed))
    alignment_delta = lax.all_to_all(row_change, "res", split_axis=1, concat_axis=0, tiled=True)
    alignment_result = alignment_representation + alignment_delta
    left_matrix = factor_matrix(normed_alignment, float_mask, first_operand_coeffs)
    right_matrix = factor_matrix(normed_alignment, float_mask, other_operand_coeffs)
    right_all, mask_all = (
        lax.all_gather(right_matrix, "res", axis=0, tiled=True),
        lax.all_gather(mask_rows, "res", axis=0, tiled=True),
    )
    update = lax.cond(
        alignment_present_flag,
        lambda: outer_block(left_matrix, mask_rows, right_all, mask_all, outer_output_weight),
        lambda: jnp.zeros(update_dimensions, jnp.float32),
    )
    update = spread(update, "branch", 0)
    pair_one = pairwise_state + update
    normed_one = layer_normalize(pair_one)
    start_rows = jnp.einsum("ijc,ch->hij", normed_one, starting_bias_weight, precision=highest)
    start_full, live_float = (
        lax.all_gather(start_rows, "res", axis=1, tiled=True),
        lax.all_gather(residue_present_mask.astype(jnp.float32), "res", axis=0, tiled=True),
    )
    live_keys = live_float > 0.5

    def starting():
        query_matrix = linear_project(normed_one, starting_projection_weight[0])
        key_matrix = linear_project(normed_one, starting_projection_weight[1])
        value_matrix = linear_project(normed_one, starting_projection_weight[2])
        gate_matrix = linear_project(normed_one, starting_projection_weight[3])

        def starting_one_row(operands):
            return attend(
                operands[0], operands[1], operands[2], operands[3], start_full, live_keys, HEADS_Z
            )

        gated_output = lax.map(
            starting_one_row, (query_matrix, key_matrix, value_matrix, gate_matrix)
        )
        return pair_one + linear_project(gated_output, starting_output_weight)

    pairwise_second = lax.cond(alignment_present_flag, lambda: jnp.zeros_like(pair_one), starting)
    normed_two = layer_normalize(pairwise_second)
    end_rows = jnp.einsum("ijc,ch->hij", normed_two, ending_bias_weight, precision=highest)
    end_full = lax.all_gather(end_rows, "res", axis=1, tiled=True)
    end_score = jnp.transpose(end_full, (0, 2, 1))
    normed_cols = lax.all_to_all(normed_two, "res", split_axis=1, concat_axis=0, tiled=True)
    column_shape = normed_cols.shape

    def ending():
        ending_q, ending_k, ending_v, ending_g = (
            linear_project(normed_cols, ending_projection_weight[0]),
            linear_project(normed_cols, ending_projection_weight[1]),
            linear_project(normed_cols, ending_projection_weight[2]),
            linear_project(normed_cols, ending_projection_weight[3]),
        )

        def one_column(column, buffer):
            result = attend(
                lax.dynamic_index_in_dim(ending_q, column, 1, keepdims=False),
                lax.dynamic_index_in_dim(ending_k, column, 1, keepdims=False),
                lax.dynamic_index_in_dim(ending_v, column, 1, keepdims=False),
                lax.dynamic_index_in_dim(ending_g, column, 1, keepdims=False),
                end_score,
                live_keys,
                HEADS_Z,
            )
            return lax.dynamic_update_index_in_dim(buffer, result, column, 1)

        gated_cols = lax.fori_loop(0, ending_q.shape[1], one_column, jnp.zeros_like(ending_q))
        return linear_project(gated_cols, ending_output_weight)

    ending_delta = lax.cond(
        alignment_present_flag, lambda: jnp.zeros(column_shape, jnp.float32), ending
    )
    pair_delta = lax.all_to_all(ending_delta, "res", split_axis=0, concat_axis=1, tiled=True)
    pairwise_result = pairwise_second + pair_delta
    sequence_halves = sequence_count // 2
    halved_width = pair_width // 2
    selected_alignment, selected_pairwise = partner(
        (alignment_result[sequence_halves:], pairwise_result[:, :, :halved_width]), "branch", 0
    )
    closing_alignment = jnp.where(
        alignment_present_flag, alignment_result[:sequence_halves], selected_alignment
    )
    final_pairwise = jnp.where(
        alignment_present_flag, selected_pairwise, pairwise_result[:, :, halved_width:]
    )
    return (closing_alignment, final_pairwise)


def solution(mesh):
    in_specs = (
        P(None, "res", None),
        P("res", None, None),
        P(None, "res"),
        P("res"),
        P(),
        P(),
        P(),
        P(),
        P(),
        P(),
        P(),
        P(),
        P(),
        P(),
        P(),
        P(),
    )
    out_specs = (P("branch", "res", None), P("res", None, "branch"))
    return jax.shard_map(
        per_device, mesh=mesh, in_specs=in_specs, out_specs=out_specs, check_vma=False
    )
```

profile of v0, /device:TPU:0, one launch (start us, length us, event | category | flops | bytes accessed | tf_op | source)
XLA Modules:
  0.0 355.1 jit_solution(5219426426211909906)
XLA Ops:
  8.8 1.8 fusion.82
  12.4 2.9 fusion.79
  16.0 7.4 %all-to-all-start.1 = ((f32[16,8,6]{1,2,0:T(8,128)}), f32[16,8,6]{1,2,0:T(8,128)}, u32[]{:S(2)}, u32[]{:S(2)}) async-start(f32[16,8,6]{1,2,0:T(8,128)} %copy.256), calls=%async_computation.1 | async-start | bytes 131072 | tf_op jit(solution)/shard_map/all_to_all | solution.py:117
  24.8 21.9 %all-gather = f32[16,6,128]{2,1,0:T(8,128)S(1)} all-gather(f32[1,6,128]{2,1,0:T(8,128)S(1)} %get-tuple-element.724), channel_id=1, replica_groups=mesh['branch'=2,'res'=16] {'res'}, dimensions={0}, use_global_device_ids=true | all-gather | bytes 52224 | tf_op jit(solution)/shard_map/all_gather | solution.py:150
  46.7 2.2 convolution_bitcast_fusion.4
  48.9 8.9 %all-gather.3.cloned.1.call-done = f32[96,32,128]{2,1,0:T(8,128)} async-done(((f32[6,32,128]{2,1,0:T(8,128)}), f32[96,32,128]{2,1,0:T(8,128)}) %all-gather.3.cloned.1.call-update) | async-done | bytes 1572880 | tf_op jit(solution)/shard_map/all_gather | solution.py:149
  57.8 35.2 %conditional.7 = (f32[6,96,128]{2,1,0:T(8,128)}) conditional(s32[]{:T(128)} %convert_element_type.6, () %tuple.72, (f32[6,128]{1,0:T(8,128)S(1)}, f32[6,32,128]{2,1,0:T(8,128)S(1)}, f32[96,32,128]{2,1,0:T(8,128)}, f32[1024,128]{1,0:T(8,128)S(1)}, f32[16,6,128]{2,1,0:T(8,128)S(1)}) %tuple.207), branch_computations={%region_13.14_spmd, %region_14.17_spmd} | conditional | flops 302174304 | bytes 7230381 | solution.py:152
  57.8 2.4 copy.264
  60.2 32.8 %while.40 = (s32[]{:T(128)}, f32[6,96,128]{2,1,0:T(8,128)}, f32[6,32,128]{2,1,0:T(8,128)S(1)}, f32[96,32,128]{2,0,1:T(8,128)S(1)}, f32[1024,128]{1,0:T(8,128)S(1...) while((s32[]{:T(128)}, f32[6,96,128]{2,1,0:T(8,128)}, f32[6,32,128]{2,1,0:T(8,128)S(1)}, ...), condition=%wide.region_16.16_spmd, body=%wide.region_15.15_spmd.sunk | while | flops 302149728 | bytes 3786589 | solution.py:72
  60.2 3.3 convolution_bitcast_fusion.8
  64.0 1.7 fusion.173
  65.7 3.3 convolution_bitcast_fusion.8
  69.5 1.7 fusion.173
  71.1 3.3 convolution_bitcast_fusion.8
  74.9 1.7 fusion.173
  76.6 3.3 convolution_bitcast_fusion.8
  80.4 1.7 fusion.173
  82.1 3.3 convolution_bitcast_fusion.8
  85.8 1.7 fusion.173
  87.5 3.3 convolution_bitcast_fusion.8
  91.3 1.7 fusion.173
  93.0 1.7 broadcast_select_fusion
  94.8 31.4 %all-reduce = f32[96]{0:T(128)S(1)} all-reduce(f32[96]{0:T(128)S(1)} %convert_dynamic-update-slice_fusion), channel_id=1, replica_groups=mesh['branch'=2,'res'=16] {'res'}, use_global_device_ids=true, to_apply=%add | all-reduce | flops 96 | bytes 768
  127.7 3.8 %all-to-all-start = ((f32[128,6,256]{2,1,0:T(8,128)}), f32[128,6,256]{2,1,0:T(8,128)S(1)}, u32[]{:S(2)}, u32[]{:S(2)}) async-start(f32[128,6,256]{2,1,0:T(8,128)} %fusion.80), calls=%async_computation | async-start | bytes 2097152 | tf_op jit(solution)/shard_map/all_to_all | solution.py:116
  132.4 33.2 %all_gather.22 = f32[4,96,96]{2,0,1:T(4,128)S(1)} all-gather(f32[4,6,96]{2,0,1:T(4,128)S(1)} %convolution_bitcast_fusion.6), channel_id=1, replica_groups=mesh['branch'=2,'res'=16] {'res'}, dimensions={1}, use_global_device_ids=true | all-gather | bytes 156672 | tf_op jit(solution)/shard_map/all_gather | solution.py:162
  167.3 5.9 %all-to-all-start.3 = ((f32[6,96,128]{2,0,1:T(8,128)}), f32[6,96,128]{2,0,1:T(8,128)}, u32[]{:S(2)}, u32[]{:S(2)}) async-start(f32[6,96,128]{2,0,1:T(8,128)} %fusion.85), calls=%async_computation.3 | async-start | bytes 786432 | tf_op jit(solution)/shard_map/all_to_all | solution.py:188
  173.2 33.9 %psum.14 = f32[8,6,96]{2,0,1:T(8,128)S(1)} all-reduce(f32[8,6,96]{2,0,1:T(8,128)S(1)} %broadcast_select_fusion.1), channel_id=1, replica_groups=mesh['branch'=2,'res'=16] {'branch'}, use_global_device_ids=true, to_apply=%region_6.7 | all-reduce | flops 4608 | bytes 36864 | tf_op jit(solution)/shard_map/psum | solution.py:16
  207.2 22.8 %all_gather.18 = f32[8,96,96]{2,0,1:T(8,128)S(1)} all-gather(f32[8,6,96]{2,0,1:T(8,128)S(1)} %psum.14), channel_id=1, replica_groups=mesh['branch'=2,'res'=16] {'res'}, dimensions={1}, use_global_device_ids=true | all-gather | bytes 313344 | tf_op jit(solution)/shard_map/all_gather | solution.py:114
  231.1 53.1 %conditional.6 = (f32[8,96,256]{2,1,0:T(8,128)S(1)}) conditional(s32[]{:T(128)} %convert_element_type.6, () %tuple.68, (f32[4,256,256]{2,1,0:T(8,128)}, f32[8,16,6,256]{3,0,1,2:T(8,128)}, f32[8,16,6]{0,2,1:T(8,128)}, f32[8,96,96]{2,0,1:T(8,128)S(1)}, f32[256,256]{1,0:T(8,128)}) %tuple.209), branch_computations={%region_7.8_spmd, %region_8.13_spmd} | conditional | flops 3077209344 | bytes 19131672 | solution.py:143
  233.9 2.3 fusion.14
  236.1 2.3 fusion.16
  238.4 2.3 fusion.18
  242.0 39.1 %while.39 = (s32[]{:T(128)}, f32[8,96,256]{1,2,0:T(8,128)}, f32[8,96,256]{1,2,0:T(8,128)}, f32[8,96,256]{1,2,0:T(8,128)}, pred[8,96]{1,0:T(8,128)(4,1)S(1)}, /*i...) while((s32[]{:T(128)}, f32[8,96,256]{1,2,0:T(8,128)}, ...), condition=%wide.region_12.12_spmd, body=%wide.region_9.11_spmd.sunk | while | flops 57309696 | bytes 2539401 | solution.py:138
  245.4 1.6 constant_dynamic-update-slice_fusion.8
  250.2 1.6 constant_dynamic-update-slice_fusion.8
  255.1 1.6 constant_dynamic-update-slice_fusion.8
  260.0 1.6 constant_dynamic-update-slice_fusion.8
  264.9 1.6 constant_dynamic-update-slice_fusion.8
  269.8 1.6 constant_dynamic-update-slice_fusion.8
  274.7 1.6 constant_dynamic-update-slice_fusion.8
  279.6 1.6 constant_dynamic-update-slice_fusion.8
  281.2 3.0 fusion.20
  285.6 3.7 %all-to-all-start.2 = ((f32[8,96,256]{2,0,1:T(8,128)}), f32[8,96,256]{2,0,1:T(8,128)S(1)}, u32[]{:S(2)}, u32[]{:S(2)}) async-start(f32[8,96,256]{2,0,1:T(8,128)} %copy.260), calls=%async_computation.2 | async-start | bytes 1572864 | tf_op jit(solution)/shard_map/all_to_all | solution.py:144
  289.4 1.6 convolution_bitcast_fusion.5
  291.0 28.1 %all_gather.23 = f32[4,96,96]{2,0,1:T(4,128)S(1)} all-gather(f32[4,6,96]{2,0,1:T(4,128)S(1)} %convolution_bitcast_fusion.5), channel_id=1, replica_groups=mesh['branch'=2,'res'=16] {'res'}, dimensions={1}, use_global_device_ids=true | all-gather | bytes 156672 | tf_op jit(solution)/shard_map/all_gather | solution.py:186
  321.5 4.5 %all-to-all-start.4 = ((f32[96,6,128]{2,1,0:T(8,128)}), f32[96,6,128]{2,1,0:T(8,128)S(1)}, u32[]{:S(2)}, u32[]{:S(2)}) async-start(f32[96,6,128]{2,1,0:T(8,128)} %copy.274), calls=%async_computation.4 | async-start | bytes 786432 | tf_op jit(solution)/shard_map/all_to_all | solution.py:217
  327.1 11.0 %all-to-all-done.4 = f32[96,6,128]{2,1,0:T(8,128)S(1)} async-done(((f32[96,6,128]{2,1,0:T(8,128)}), f32[96,6,128]{2,1,0:T(8,128)S(1)}, u32[]{:S(2)}, u32[]{:S(2)}) %all-to-all-start.4) | async-done | bytes 294944 | tf_op jit(solution)/shard_map/all_to_all | solution.py:217
  339.3 8.0 %collective-permute-done.1 = f32[6,96,64]{2,1,0:T(8,128)S(1)} collective-permute-done((f32[6,96,64]{2,1,0:T(8,128)S(1)}, f32[6,96,64]{2,1,0:T(8,128)S(1)}, u32[]{:S(2)}, u32[]{:S(2)}) %collective-permute-start.1) | collective-permute-done | bytes 147488 | tf_op jit(solution)/shard_map/ppermute | solution.py:26
  (165 shorter events, 49.8 us)
Async XLA Ops:
  7.2 5.2 %copy-start = (f32[256,32]{0,1:T(8,128)S(1)}, f32[256,32]{0,1:T(8,128)}, u32[]{:S(2)}) copy-start(f32[256,32]{0,1:T(8,128)} %param.42) | copy-start | bytes 98308
  7.2 3.6 %copy-start.2 = (f32[128,6,256]{2,0,1:T(8,128)S(1)}, f32[128,6,256]{2,0,1:T(8,128)}, u32[]{:S(2)}) copy-start(f32[128,6,256]{2,0,1:T(8,128)} %param.34) | copy-start | bytes 2359300
  7.2 50.6 %all-gather.3.cloned.1.call-start = ((), (), s32[]{:S(2)}) async-start(), calls=%async_computation.5 | async-start | bytes 1671168 | tf_op jit(solution)/shard_map/all_gather | solution.py:149
  8.6 3.7 %copy-start.12 = (s32[128,6]{0,1:T(8,128)S(1)}, s32[128,6]{0,1:T(8,128)}, u32[]{:S(2)}) copy-start(s32[128,6]{0,1:T(8,128)} %param.36) | copy-start | bytes 9220
  10.8 12.7 %copy-start.17 = (u32[32]{0:T(128)S(1)}, u32[32]{0:T(128)}, u32[]{:S(2)}) copy-start(u32[32]{0:T(128)} %constant.198) | copy-start | bytes 388
  10.8 35.9 %copy-start.11 = (f32[256,32]{0,1:T(8,128)S(1)}, f32[256,32]{0,1:T(8,128)}, u32[]{:S(2)}) copy-start(f32[256,32]{0,1:T(8,128)} %param.41) | copy-start | bytes 98308
  12.4 45.4 %copy-start.1 = (f32[1024,128]{1,0:T(8,128)S(1)}, f32[1024,128]{1,0:T(8,128)}, u32[]{:S(2)}) copy-start(f32[1024,128]{1,0:T(8,128)} %param.43) | copy-start | bytes 1572868
  16.0 111.7 %all-to-all-start.1 = ((f32[16,8,6]{1,2,0:T(8,128)}), f32[16,8,6]{1,2,0:T(8,128)}, u32[]{:S(2)}, u32[]{:S(2)}) async-start(f32[16,8,6]{1,2,0:T(8,128)} %copy.256), calls=%async_computation.1 | async-start | bytes 131072 | tf_op jit(solution)/shard_map/all_to_all | solution.py:117
  23.4 102.8 %all-reduce.3.cloned.1.call-start = ((), (), s32[]{:S(2)}) async-start(), calls=%async_computation.6 | async-start | bytes 589824 | tf_op jit(solution)/shard_map/psum | solution.py:16
  57.8 36.9 %copy-start.16 = (s32[6]{0:T(128)S(1)}, s32[6]{0:T(128)}, u32[]{:S(2)}) copy-start(s32[6]{0:T(128)} %param.37) | copy-start | bytes 76
  57.8 68.4 %copy-start.3 = (f32[6,96,128]{2,1,0:T(8,128)S(1)}, f32[6,96,128]{2,1,0:T(8,128)}, u32[]{:S(2)}) copy-start(f32[6,96,128]{2,1,0:T(8,128)} %param.35) | copy-start | bytes 884740
  127.4 4.4 %copy-start.14 = (f32[128,4]{0,1:T(4,128)S(1)}, f32[128,4]{0,1:T(4,128)}, u32[]{:S(2)}) copy-start(f32[128,4]{0,1:T(4,128)} %param.45) | copy-start | bytes 6148
  127.7 37.9 %copy-start.7 = (f32[4,128,128]{2,1,0:T(8,128)S(1)}, f32[4,128,128]{2,1,0:T(8,128)}, u32[]{:S(2)}) copy-start(f32[4,128,128]{2,1,0:T(8,128)} %param.44) | copy-start | bytes 786436
  127.7 37.9 %copy-start.9 = (f32[128,128]{1,0:T(8,128)S(1)}, f32[128,128]{1,0:T(8,128)}, u32[]{:S(2)}) copy-start(f32[128,128]{1,0:T(8,128)} %param.46) | copy-start | bytes 196612
  127.7 39.6 %all-to-all-start = ((f32[128,6,256]{2,1,0:T(8,128)}), f32[128,6,256]{2,1,0:T(8,128)S(1)}, u32[]{:S(2)}, u32[]{:S(2)}) async-start(f32[128,6,256]{2,1,0:T(8,128)} %fusion.80), calls=%async_computation | async-start | bytes 2097152 | tf_op jit(solution)/shard_map/all_to_all | solution.py:116
  165.6 7.6 %copy-start.13 = (f32[128,8]{0,1:T(8,128)S(1)}, f32[128,8]{0,1:T(8,128)}, u32[]{:S(2)}) copy-start(f32[128,8]{0,1:T(8,128)} %param.40) | copy-start | bytes 12292
  167.3 118.3 %all-to-all-start.3 = ((f32[6,96,128]{2,0,1:T(8,128)}), f32[6,96,128]{2,0,1:T(8,128)}, u32[]{:S(2)}, u32[]{:S(2)}) async-start(f32[6,96,128]{2,0,1:T(8,128)} %fusion.85), calls=%async_computation.3 | async-start | bytes 786432 | tf_op jit(solution)/shard_map/all_to_all | solution.py:188
  231.1 1.5 copy-start.6
  242.0 39.2 %copy-start.8 = (f32[256,256]{1,0:T(8,128)S(1)}, f32[256,256]{1,0:T(8,128)}, u32[]{:S(2)}) copy-start(f32[256,256]{1,0:T(8,128)} %get-tuple-element.359) | copy-start | bytes 786436 | tf_op jit(solution)/shard_map/cond
  284.2 5.1 %copy-start.15 = (f32[128,4]{0,1:T(4,128)S(1)}, f32[128,4]{0,1:T(4,128)}, u32[]{:S(2)}) copy-start(f32[128,4]{0,1:T(4,128)} %param.48) | copy-start | bytes 6148
  285.6 34.6 %copy-start.10 = (f32[128,128]{1,0:T(8,128)S(1)}, f32[128,128]{1,0:T(8,128)}, u32[]{:S(2)}) copy-start(f32[128,128]{1,0:T(8,128)} %param.49) | copy-start | bytes 196612
  285.6 35.9 %all-to-all-start.2 = ((f32[8,96,256]{2,0,1:T(8,128)}), f32[8,96,256]{2,0,1:T(8,128)S(1)}, u32[]{:S(2)}, u32[]{:S(2)}) async-start(f32[8,96,256]{2,0,1:T(8,128)} %copy.260), calls=%async_computation.2 | async-start | bytes 1572864 | tf_op jit(solution)/shard_map/all_to_all | solution.py:144
  321.5 16.6 %all-to-all-start.4 = ((f32[96,6,128]{2,1,0:T(8,128)}), f32[96,6,128]{2,1,0:T(8,128)S(1)}, u32[]{:S(2)}, u32[]{:S(2)}) async-start(f32[96,6,128]{2,1,0:T(8,128)} %copy.274), calls=%async_computation.4 | async-start | bytes 786432 | tf_op jit(solution)/shard_map/all_to_all | solution.py:217
  326.1 0.9 copy-start.4
  327.0 11.5 %copy-start.5 = (f32[128,6,256]{2,0,1:T(8,128)S(1)}, f32[128,6,256]{2,0,1:T(8,128)}, u32[]{:S(2)}) copy-start(f32[128,6,256]{2,0,1:T(8,128)} %copy-done.4) | copy-start | bytes 2359300
  327.0 11.5 %collective-permute-start = (f32[64,6,256]{2,0,1:T(8,128)S(1)}, f32[64,6,256]{2,0,1:T(8,128)S(1)}, u32[]{:S(2)}, u32[]{:S(2)}) collective-permute-start(f32[64,6,256]{2,0,1:T(8,128)S(1)} %slice.53), channel_id=1, source_target_pairs={{0,16},{16,0},{1,17},{17,1},{2,18},{18,2},{3,19},{19,3},{4,20},{20... | collective-permute-start | bytes 1179656 | tf_op jit(solution)/shard_map/ppermute | solution.py:26
  338.2 9.1 %collective-permute-start.1 = (f32[6,96,64]{2,1,0:T(8,128)S(1)}, f32[6,96,64]{2,1,0:T(8,128)S(1)}, u32[]{:S(2)}, u32[]{:S(2)}) collective-permute-start(f32[6,96,64]{2,1,0:T(8,128)S(1)} %bitcast.264), channel_id=1, source_target_pairs={{0,16},{16,0},{1,17},{17,1},{2,18},{18,2},{3,19},{19,3},{4,20},{20... | collective-permute-start | bytes 442376 | tf_op jit(solution)/shard_map/ppermute | solution.py:26
Sparse Core Ops, SparseCore 0:
  15.4 42.3 all-gather.2
  94.8 21.5 all-reduce.2
where the time goes:
time: 357 us; the launch traced here: 355 us
  blocking collectives  171 us (48%)
  matrix products  59.8 us (17%)
  local copies, waits for them, and re-layouts  30.1 us (8%)
  waiting for transfers between devices  28.2 us (8%)
  starting transfers between devices  25.5 us (7%)
  other arithmetic  24.2 us (7%)
  between operations  15.1 us (4%)
    psum x1, blocking collectives, spread(): return lax.psum(jnp.where(mine, value, jnp.zeros_like(value)), axis)  33.9 us
    all_gather x1, blocking collectives, per_device(): lax.all_gather(start_rows, 'res', axis=1, tiled=True)  33.2 us
    unnamed x1, blocking collectives  31.4 us
    all_gather x1, blocking collectives, per_device(): end_full = lax.all_gather(end_rows, 'res', axis=1, tiled=True)  28.1 us
    dot_general x13, matrix products, linear_project(): jnp.dot(values, weight, precision=highest, preferred_element_type=jnp.flo...  26.3 us
    all_gather x1, blocking collectives, per_device(): row_bias = lax.all_gather(own_rows, 'res', axis=1, tiled=True)  22.8 us
    all_gather x1, blocking collectives, per_device(): lax.all_gather(mask_rows, 'res', axis=0, tiled=True)  21.9 us
    dot_general x6, matrix products, outer_one_row(): jnp.einsum('cs,jes->jce', row_left, right_all, precision=highest)  19.8 us
  transfers between devices with their start and end apart: 9, of which 4 were waited for; matrix products, arithmetic and copies ran while one was open for 29% of the time, Pallas kernels for 0%

commit v1 on v0

--- a/solution.py
+++ b/solution.py
@@ -183,7 +183,13 @@
     pairwise_second = lax.cond(alignment_present_flag, lambda: jnp.zeros_like(pair_one), starting)
     normed_two = layer_normalize(pairwise_second)
     end_rows = jnp.einsum("ijc,ch->hij", normed_two, ending_bias_weight, precision=highest)
-    end_full = lax.all_gather(end_rows, "res", axis=1, tiled=True)
+
+    def _edit_outputs(in_array):
+        carry = lax.all_gather(in_array, "res")
+        res = jnp.concatenate(carry, 1)
+        return res
+
+    end_full = _edit_outputs(end_rows)
     end_score = jnp.transpose(end_full, (0, 2, 1))
     normed_cols = lax.all_to_all(normed_two, "res", split_axis=1, concat_axis=0, tiled=True)
     column_shape = normed_cols.shape

time: 357 us -> 350 us (0.980)
  blocking collectives: 171 us -> 167 us
    psum x1, blocking collectives: 33.9 us -> 26.7 us  [spread(): return lax.psum(jnp.where(mine, value, jnp.zeros_like(value)), axis)]
  transfers between devices with their start and end apart: 9 -> 9, of which waited for: 4 -> 3; matrix products, arithmetic and copies ran while one was open for 29% -> 29% of each run, Pallas kernels for 0% -> 0%
where the time goes in v1:
time: 350 us; the launch traced here: 348 us
  blocking collectives  167 us (48%)
  matrix products  60 us (17%)
  local copies, waits for them, and re-layouts  27.9 us (8%)
  waiting for transfers between devices  27.6 us (8%)
  starting transfers between devices  25.4 us (7%)
  other arithmetic  24.2 us (7%)
  between operations  15.1 us (4%)
    all_gather x1, blocking collectives, per_device(): lax.all_gather(start_rows, 'res', axis=1, tiled=True)  34.6 us
    unnamed x1, blocking collectives  31.4 us
    all_gather x1, blocking collectives, _edit_outputs(): carry = lax.all_gather(in_array, 'res')  28.4 us
    psum x1, blocking collectives, spread(): return lax.psum(jnp.where(mine, value, jnp.zeros_like(value)), axis)  26.7 us
    dot_general x13, matrix products, linear_project(): jnp.dot(values, weight, precision=highest, preferred_element_type=jnp.flo...  26.4 us
    all_gather x1, blocking collectives, per_device(): lax.all_gather(mask_rows, 'res', axis=0, tiled=True)  23.4 us
    all_gather x1, blocking collectives, per_device(): row_bias = lax.all_gather(own_rows, 'res', axis=1, tiled=True)  22.9 us
    dot_general x6, matrix products, outer_one_row(): jnp.einsum('cs,jes->jce', row_left, right_all, precision=highest)  19.8 us
  transfers between devices with their start and end apart: 9, of which 3 were waited for; matrix products, arithmetic and copies ran while one was open for 29% of the time, Pallas kernels for 0%

profile of v1, /device:TPU:0, one launch (start us, length us, event | category | flops | bytes accessed | tf_op | source)
XLA Modules:
  0.0 348.4 jit_solution(8234035048731064037)
XLA Ops:
  8.8 1.8 fusion.82
  12.4 2.9 fusion.79
  16.0 7.4 %all-to-all-start.1 = ((f32[16,8,6]{1,2,0:T(8,128)}), f32[16,8,6]{1,2,0:T(8,128)}, u32[]{:S(2)}, u32[]{:S(2)}) async-start(f32[16,8,6]{1,2,0:T(8,128)} %copy.263), calls=%async_computation.1 | async-start | bytes 131072 | tf_op jit(solution)/shard_map/all_to_all | solution.py:117
  24.7 23.4 %all-gather.1 = f32[16,6,128]{2,1,0:T(8,128)} all-gather(f32[1,6,128]{2,1,0:T(8,128)S(1)} %get-tuple-element.719), channel_id=1, replica_groups=mesh['branch'=2,'res'=16] {'res'}, dimensions={0}, use_global_device_ids=true | all-gather | bytes 52224 | tf_op jit(solution)/shard_map/all_gather | solution.py:150
  48.2 2.2 convolution_bitcast_fusion.4
  50.4 7.4 %all-gather.4.cloned.1.call-done = f32[96,32,128]{2,1,0:T(8,128)} async-done(((f32[6,32,128]{2,1,0:T(8,128)}), f32[96,32,128]{2,1,0:T(8,128)}) %all-gather.4.cloned.1.call-update) | async-done | bytes 1572880 | tf_op jit(solution)/shard_map/all_gather | solution.py:149
  57.8 35.2 %conditional.7 = (f32[6,96,128]{2,1,0:T(8,128)}) conditional(s32[]{:T(128)} %convert_element_type.6, () %tuple.72, (f32[6,128]{1,0:T(8,128)S(1)}, f32[6,32,128]{2,1,0:T(8,128)S(1)}, f32[96,32,128]{2,1,0:T(8,128)}, f32[1024,128]{1,0:T(8,128)S(1)}, f32[16,6,128]{2,1,0:T(8,128)}) %tuple.206), branch_computations={%region_13.14_spmd, %region_14.17_spmd} | conditional | flops 302174304 | bytes 7427017 | solution.py:152
  57.8 2.4 copy.271
  60.2 32.8 %while.40 = (s32[]{:T(128)}, f32[6,96,128]{2,1,0:T(8,128)}, f32[6,32,128]{2,1,0:T(8,128)S(1)}, f32[96,32,128]{2,0,1:T(8,128)S(1)}, f32[1024,128]{1,0:T(8,128)S(1...) while((s32[]{:T(128)}, f32[6,96,128]{2,1,0:T(8,128)}, f32[6,32,128]{2,1,0:T(8,128)S(1)}, ...), condition=%wide.region_16.16_spmd, body=%wide.region_15.15_spmd.sunk | while | flops 302149728 | bytes 3786589 | solution.py:72
  60.3 3.3 convolution_bitcast_fusion.8
  64.0 1.7 fusion.173
  65.7 3.3 convolution_bitcast_fusion.8
  69.5 1.7 fusion.173
  71.2 3.3 convolution_bitcast_fusion.8
  75.0 1.7 fusion.173
  76.6 3.3 convolution_bitcast_fusion.8
  80.4 1.7 fusion.173
  82.1 3.3 convolution_bitcast_fusion.8
  85.9 1.7 fusion.173
  87.6 3.3 convolution_bitcast_fusion.8
  91.3 1.7 fusion.173
  93.0 1.7 broadcast_select_fusion
  94.9 31.4 %all-reduce = f32[96]{0:T(128)S(1)} all-reduce(f32[96]{0:T(128)S(1)} %convert_dynamic-update-slice_fusion), channel_id=1, replica_groups=mesh['branch'=2,'res'=16] {'res'}, use_global_device_ids=true, to_apply=%add | all-reduce | flops 96 | bytes 768
  127.7 3.7 %all-to-all-start = ((f32[128,6,256]{2,1,0:T(8,128)}), f32[128,6,256]{2,1,0:T(8,128)S(1)}, u32[]{:S(2)}, u32[]{:S(2)}) async-start(f32[128,6,256]{2,1,0:T(8,128)} %fusion.80), calls=%async_computation | async-start | bytes 2097152 | tf_op jit(solution)/shard_map/all_to_all | solution.py:116
  132.3 34.6 %all_gather.25 = f32[4,96,96]{2,0,1:T(4,128)} all-gather(f32[4,6,96]{2,0,1:T(4,128)S(1)} %convolution_bitcast_fusion.6), channel_id=1, replica_groups=mesh['branch'=2,'res'=16] {'res'}, dimensions={1}, use_global_device_ids=true | all-gather | bytes 156672 | tf_op jit(solution)/shard_map/all_gather | solution.py:162
  168.6 5.8 %all-to-all-start.3 = ((f32[6,96,128]{2,0,1:T(8,128)}), f32[6,96,128]{2,0,1:T(8,128)S(1)}, u32[]{:S(2)}, u32[]{:S(2)}) async-start(f32[6,96,128]{2,0,1:T(8,128)} %fusion.85), calls=%async_computation.3 | async-start | bytes 786432 | tf_op jit(solution)/shard_map/all_to_all | solution.py:194
  174.4 26.7 %psum.14 = f32[8,6,96]{2,0,1:T(8,128)S(1)} all-reduce(f32[8,6,96]{2,0,1:T(8,128)S(1)} %broadcast_select_fusion.1), channel_id=1, replica_groups=mesh['branch'=2,'res'=16] {'branch'}, use_global_device_ids=true, to_apply=%region_6.7 | all-reduce | flops 4608 | bytes 36864 | tf_op jit(solution)/shard_map/psum | solution.py:16
  201.2 22.9 %all_gather.21 = f32[8,96,96]{2,0,1:T(8,128)S(1)} all-gather(f32[8,6,96]{2,0,1:T(8,128)S(1)} %psum.14), channel_id=1, replica_groups=mesh['branch'=2,'res'=16] {'res'}, dimensions={1}, use_global_device_ids=true | all-gather | bytes 313344 | tf_op jit(solution)/shard_map/all_gather | solution.py:114
  224.3 53.2 %conditional.6 = (f32[8,96,256]{2,1,0:T(8,128)S(1)}) conditional(s32[]{:T(128)} %convert_element_type.6, () %tuple.68, (f32[4,256,256]{2,1,0:T(8,128)}, f32[8,16,6,256]{3,0,1,2:T(8,128)S(1)}, f32[8,16,6]{0,2,1:T(8,128)}, f32[8,96,96]{2,0,1:T(8,128)S(1)}, f32[256,256]{1,0:T(8,128)}) %tuple.208), branch_computations={%region_7.8_spmd, %region_8.13_spmd} | conditional | flops 3077209344 | bytes 19131672 | solution.py:143
  227.1 2.3 fusion.14
  229.4 2.3 fusion.16
  231.7 2.3 fusion.18
  235.4 39.1 %while.39 = (s32[]{:T(128)}, f32[8,96,256]{1,2,0:T(8,128)}, f32[8,96,256]{1,2,0:T(8,128)}, f32[8,96,256]{1,2,0:T(8,128)}, pred[8,96]{1,0:T(8,128)(4,1)S(1)}, /*i...) while((s32[]{:T(128)}, f32[8,96,256]{1,2,0:T(8,128)}, ...), condition=%wide.region_12.12_spmd, body=%wide.region_9.11_spmd.sunk | while | flops 57309696 | bytes 2539401 | solution.py:138
  238.7 1.6 constant_dynamic-update-slice_fusion.8
  243.6 1.6 constant_dynamic-update-slice_fusion.8
  248.5 1.6 constant_dynamic-update-slice_fusion.8
  253.3 1.6 constant_dynamic-update-slice_fusion.8
  258.2 1.6 constant_dynamic-update-slice_fusion.8
  263.1 1.6 constant_dynamic-update-slice_fusion.8
  268.0 1.6 constant_dynamic-update-slice_fusion.8
  272.9 1.6 constant_dynamic-update-slice_fusion.8
  274.5 3.0 fusion.20
  278.9 3.7 %all-to-all-start.2 = ((f32[8,96,256]{2,0,1:T(8,128)}), f32[8,96,256]{2,0,1:T(8,128)S(1)}, u32[]{:S(2)}, u32[]{:S(2)}) async-start(f32[8,96,256]{2,0,1:T(8,128)} %copy.267), calls=%async_computation.2 | async-start | bytes 1572864 | tf_op jit(solution)/shard_map/all_to_all | solution.py:144
  282.7 1.6 convolution_bitcast_fusion.5
  284.3 28.4 %all-gather = f32[64,6,96]{2,1,0:T(8,128)S(1)} all-gather(f32[4,6,96]{2,1,0:T(8,128)S(1)} %copy.279), channel_id=2, replica_groups=mesh['branch'=2,'res'=16] {'res'}, dimensions={0}, use_global_device_ids=true | all-gather | bytes 156672 | tf_op jit(solution)/shard_map/all_gather | solution.py:188
  314.8 4.5 %all-to-all-start.4 = ((f32[96,6,128]{2,1,0:T(8,128)}), f32[96,6,128]{2,1,0:T(8,128)S(1)}, u32[]{:S(2)}, u32[]{:S(2)}) async-start(f32[96,6,128]{2,1,0:T(8,128)} %copy.283), calls=%async_computation.4 | async-start | bytes 786432 | tf_op jit(solution)/shard_map/all_to_all | solution.py:223
  319.5 11.9 %all-to-all-done.4 = f32[96,6,128]{2,1,0:T(8,128)S(1)} async-done(((f32[96,6,128]{2,1,0:T(8,128)}), f32[96,6,128]{2,1,0:T(8,128)S(1)}, u32[]{:S(2)}, u32[]{:S(2)}) %all-to-all-start.4) | async-done | bytes 294944 | tf_op jit(solution)/shard_map/all_to_all | solution.py:223
  332.4 8.2 %collective-permute-done.1 = f32[6,96,64]{2,1,0:T(8,128)S(1)} collective-permute-done((f32[6,96,64]{2,1,0:T(8,128)S(1)}, f32[6,96,64]{2,1,0:T(8,128)S(1)}, u32[]{:S(2)}, u32[]{:S(2)}) %collective-permute-start.1) | collective-permute-done | bytes 147488 | tf_op jit(solution)/shard_map/ppermute | solution.py:26
  (161 shorter events, 47.4 us)
Async XLA Ops:
  7.2 5.2 %copy-start = (f32[256,32]{0,1:T(8,128)S(1)}, f32[256,32]{0,1:T(8,128)}, u32[]{:S(2)}) copy-start(f32[256,32]{0,1:T(8,128)} %param.42) | copy-start | bytes 98308
  7.2 3.6 %copy-start.2 = (f32[128,6,256]{2,0,1:T(8,128)S(1)}, f32[128,6,256]{2,0,1:T(8,128)}, u32[]{:S(2)}) copy-start(f32[128,6,256]{2,0,1:T(8,128)} %param.34) | copy-start | bytes 2359300
  7.2 50.6 %all-gather.4.cloned.1.call-start = ((), (), s32[]{:S(2)}) async-start(), calls=%async_computation.5 | async-start | bytes 1671168 | tf_op jit(solution)/shard_map/all_gather | solution.py:149
  8.6 3.7 %copy-start.9 = (s32[128,6]{0,1:T(8,128)S(1)}, s32[128,6]{0,1:T(8,128)}, u32[]{:S(2)}) copy-start(s32[128,6]{0,1:T(8,128)} %param.36) | copy-start | bytes 9220
  10.8 12.7 %copy-start.14 = (u32[32]{0:T(128)S(1)}, u32[32]{0:T(128)}, u32[]{:S(2)}) copy-start(u32[32]{0:T(128)} %constant.198) | copy-start | bytes 388
  10.8 37.4 %copy-start.8 = (f32[256,32]{0,1:T(8,128)S(1)}, f32[256,32]{0,1:T(8,128)}, u32[]{:S(2)}) copy-start(f32[256,32]{0,1:T(8,128)} %param.41) | copy-start | bytes 98308
  12.4 45.4 %copy-start.1 = (f32[1024,128]{1,0:T(8,128)S(1)}, f32[1024,128]{1,0:T(8,128)}, u32[]{:S(2)}) copy-start(f32[1024,128]{1,0:T(8,128)} %param.43) | copy-start | bytes 1572868
  16.0 111.7 %all-to-all-start.1 = ((f32[16,8,6]{1,2,0:T(8,128)}), f32[16,8,6]{1,2,0:T(8,128)}, u32[]{:S(2)}, u32[]{:S(2)}) async-start(f32[16,8,6]{1,2,0:T(8,128)} %copy.263), calls=%async_computation.1 | async-start | bytes 131072 | tf_op jit(solution)/shard_map/all_to_all | solution.py:117
  23.4 102.8 %all-reduce.3.cloned.1.call-start = ((), (), s32[]{:S(2)}) async-start(), calls=%async_computation.6 | async-start | bytes 589824 | tf_op jit(solution)/shard_map/psum | solution.py:16
  57.8 37.0 %copy-start.13 = (s32[6]{0:T(128)S(1)}, s32[6]{0:T(128)}, u32[]{:S(2)}) copy-start(s32[6]{0:T(128)} %param.37) | copy-start | bytes 76
  57.8 68.4 %copy-start.3 = (f32[6,96,128]{2,1,0:T(8,128)S(1)}, f32[6,96,128]{2,1,0:T(8,128)}, u32[]{:S(2)}) copy-start(f32[6,96,128]{2,1,0:T(8,128)} %param.35) | copy-start | bytes 884740
  57.8 2.4 copy-start.5
  127.4 4.2 %copy-start.11 = (f32[128,4]{0,1:T(4,128)S(1)}, f32[128,4]{0,1:T(4,128)}, u32[]{:S(2)}) copy-start(f32[128,4]{0,1:T(4,128)} %param.45) | copy-start | bytes 6148
  127.7 40.8 %all-to-all-start = ((f32[128,6,256]{2,1,0:T(8,128)}), f32[128,6,256]{2,1,0:T(8,128)S(1)}, u32[]{:S(2)}, u32[]{:S(2)}) async-start(f32[128,6,256]{2,1,0:T(8,128)} %fusion.80), calls=%async_computation | async-start | bytes 2097152 | tf_op jit(solution)/shard_map/all_to_all | solution.py:116
  166.9 7.5 %copy-start.10 = (f32[128,8]{0,1:T(8,128)S(1)}, f32[128,8]{0,1:T(8,128)}, u32[]{:S(2)}) copy-start(f32[128,8]{0,1:T(8,128)} %param.40) | copy-start | bytes 12292
  168.6 110.3 %all-to-all-start.3 = ((f32[6,96,128]{2,0,1:T(8,128)}), f32[6,96,128]{2,0,1:T(8,128)S(1)}, u32[]{:S(2)}, u32[]{:S(2)}) async-start(f32[6,96,128]{2,0,1:T(8,128)} %fusion.85), calls=%async_computation.3 | async-start | bytes 786432 | tf_op jit(solution)/shard_map/all_to_all | solution.py:194
  224.5 1.2 copy-start.4
  235.3 39.1 %copy-start.6 = (f32[256,256]{1,0:T(8,128)S(1)}, f32[256,256]{1,0:T(8,128)}, u32[]{:S(2)}) copy-start(f32[256,256]{1,0:T(8,128)} %get-tuple-element.359) | copy-start | bytes 786436 | tf_op jit(solution)/shard_map/cond
  277.5 5.1 %copy-start.12 = (f32[128,4]{0,1:T(4,128)S(1)}, f32[128,4]{0,1:T(4,128)}, u32[]{:S(2)}) copy-start(f32[128,4]{0,1:T(4,128)} %param.48) | copy-start | bytes 6148
  278.9 34.6 %copy-start.7 = (f32[128,128]{1,0:T(8,128)S(1)}, f32[128,128]{1,0:T(8,128)}, u32[]{:S(2)}) copy-start(f32[128,128]{1,0:T(8,128)} %param.49) | copy-start | bytes 196612
  278.9 35.9 %all-to-all-start.2 = ((f32[8,96,256]{2,0,1:T(8,128)}), f32[8,96,256]{2,0,1:T(8,128)S(1)}, u32[]{:S(2)}, u32[]{:S(2)}) async-start(f32[8,96,256]{2,0,1:T(8,128)} %copy.267), calls=%async_computation.2 | async-start | bytes 1572864 | tf_op jit(solution)/shard_map/all_to_all | solution.py:144
  314.8 16.6 %all-to-all-start.4 = ((f32[96,6,128]{2,1,0:T(8,128)}), f32[96,6,128]{2,1,0:T(8,128)S(1)}, u32[]{:S(2)}, u32[]{:S(2)}) async-start(f32[96,6,128]{2,1,0:T(8,128)} %copy.283), calls=%async_computation.4 | async-start | bytes 786432 | tf_op jit(solution)/shard_map/all_to_all | solution.py:223
  319.4 12.2 %collective-permute-start = (f32[64,6,256]{2,0,1:T(8,128)S(1)}, f32[64,6,256]{2,0,1:T(8,128)S(1)}, u32[]{:S(2)}, u32[]{:S(2)}) collective-permute-start(f32[64,6,256]{2,0,1:T(8,128)S(1)} %slice.53), channel_id=1, source_target_pairs={{0,16},{16,0},{1,17},{17,1},{2,18},{18,2},{3,19},{19,3},{4,20},{20... | collective-permute-start | bytes 1179656 | tf_op jit(solution)/shard_map/ppermute | solution.py:26
  331.5 9.1 %collective-permute-start.1 = (f32[6,96,64]{2,1,0:T(8,128)S(1)}, f32[6,96,64]{2,1,0:T(8,128)S(1)}, u32[]{:S(2)}, u32[]{:S(2)}) collective-permute-start(f32[6,96,64]{2,1,0:T(8,128)S(1)} %bitcast.270), channel_id=1, source_target_pairs={{0,16},{16,0},{1,17},{17,1},{2,18},{18,2},{3,19},{19,3},{4,20},{20... | collective-permute-start | bytes 442376 | tf_op jit(solution)/shard_map/ppermute | solution.py:26
Sparse Core Ops, SparseCore 0:
  15.4 42.3 all-gather.3
  94.9 21.5 all-reduce.2
